TPU v7x, 32 devices: a whole 2x2x4 slice. The times are simulated.
32 devices in a mesh: row: 8 (over y, x, core), col: 4 (over z).
Axes of the slice: x: 2, y: 2, z: 4, core: 2. Of those that a mesh axis runs over, the one named last changes fastest.
Arguments:
- features: float32 [4096, 128], P(('row', 'col')), may hold values from -6 to 6
- weight: float32 [128, 128], replicated, may hold values from -0.5 to 0.5
- layer_bias: float32 [128], replicated, may hold values from -3 to 3
- degree_scale: float32 [4096], P(('row', 'col')), may hold values from 0.05 to 0.5
- tile_values: bfloat16 [8, 4, 32, 128, 128], P('row', 'col'), may hold values from 0 to 1
- tile_slots: int32 [8, 4, 32], P('row', 'col'), may hold values from 0 to 31, as said below
- tile_count: int32 [8, 4], P('row', 'col'), may hold values from 1 to 32, as said below
- cotangent: float32 [4096, 128], P(('row', 'col')), may hold values from -6 to 6
Outputs:
- activations: float32 [4096, 128], P(('row', 'col'))
- feature_grad: float32 [4096, 128], P(('row', 'col'))
- weight_grad: float32 [128, 128], replicated
- bias_grad: float32 [128], replicated
Inputs may be any that keep to these rules, and one draw needn't show every extreme that they name: `tile_slots`: the first tile_count[r, c] slots of a device name distinct positions of its grid of 8 by 4 tiles (row u, column v as p = u * 4 + v); later slots hold other positions in range and are ignored. `tile_count`: counts are skewed across devices; in every draw some device has a full list of 32 tiles.
All inputs are finite; a program needn't handle non-finite values.
Results may differ from a plain program's by a relative error of at most 0.0059.
Values may be sent and summed in bfloat16 or wider, within the bound.
A program may use at most 64 MiB of HBM per device.

v0:
```python
import math
import jax
import jax.numpy as jnp
from jax import lax
from jax.sharding import PartitionSpec as P

TBLK = 32


def gelu_pair(values):
    argument = 0.7978845608028654 * (values + 0.044715 * values * values * values)
    tangent = jnp.tanh(argument)
    output = 0.5 * values * (1.0 + tangent)
    slopes = 0.5 * (1.0 + tangent) + 0.5 * values * (
        1.0 - tangent * tangent
    ) * 0.7978845608028654 * (1.0 + 3.0 * 0.044715 * values * values)
    return (output, slopes)


def aggregate(
    blocks, target_index, source_index, live_count, source, target_first, target_blocks, form
):
    tile_size = blocks.shape[1]
    feature_width = source.shape[1]
    source_blocks = source.reshape(-1, tile_size, feature_width)
    block_count = (live_count + TBLK - 1) // TBLK
    positions = target_first + jnp.arange(target_blocks, dtype=jnp.int32)

    def accumulate(block_index, totals):
        first_tile = block_index * TBLK
        tile_block = lax.dynamic_slice_in_dim(blocks, first_tile, TBLK, 0)
        targets = lax.dynamic_slice_in_dim(target_index, first_tile, TBLK, 0)
        sources = lax.dynamic_slice_in_dim(source_index, first_tile, TBLK, 0)
        picked = source_blocks[sources]
        products = jnp.einsum(form, tile_block, picked, preferred_element_type=jnp.float32)
        live_mask = first_tile + jnp.arange(TBLK, dtype=jnp.int32) < live_count
        selector = ((targets[None, :] == positions[:, None]) & live_mask[None, :]).astype(
            jnp.float32
        )
        return totals + jnp.dot(
            selector,
            products.reshape(TBLK, tile_size * feature_width),
            precision=lax.Precision.HIGHEST,
            preferred_element_type=jnp.float32,
        )

    empty = jnp.zeros((target_blocks, tile_size * feature_width), jnp.float32)
    totals = lax.fori_loop(0, block_count, accumulate, empty)
    return totals.reshape(target_blocks * tile_size, feature_width)


def local(
    features, weight, layer_bias, degree_scale, tile_values, tile_slots, tile_count, cotangent
):
    highest = lax.Precision.HIGHEST
    own_rows = features.shape[0]
    tile_size = tile_values.shape[3]
    row_devices = lax.axis_size("row")
    col_devices = lax.axis_size("col")
    local_blocks = own_rows // tile_size
    column_blocks = col_devices * local_blocks
    row_blocks = row_devices * local_blocks
    blocks = tile_values[0, 0]
    slots = tile_slots[0, 0]
    live_count = tile_count[0, 0]
    local_rows = slots // column_blocks
    local_cols = slots % column_blocks
    norm_factor = 1.0 / math.sqrt(own_rows * row_devices * col_devices)
    projected = jnp.dot(features, weight, precision=highest, preferred_element_type=jnp.float32)
    scaled = (degree_scale[:, None] * projected).astype(jnp.bfloat16)
    gathered = lax.all_gather(scaled, "col", axis=0, tiled=True)
    partial_value = aggregate(
        blocks,
        local_rows,
        local_cols,
        live_count,
        gathered,
        0 // tile_size,
        row_blocks * tile_size // tile_size,
        "tij,tjf->tif",
    )
    summed = lax.psum_scatter(partial_value, "row", scatter_dimension=0, tiled=True)
    preact = degree_scale[:, None] * summed + layer_bias[None, :]
    activation, slopes = gelu_pair(preact)
    delta = cotangent * slopes
    bias_part = jnp.sum(delta, axis=0)
    delta_scaled = (degree_scale[:, None] * delta).astype(jnp.bfloat16)
    delta_rows = lax.all_gather(delta_scaled, "row", axis=0, tiled=True)
    back_partial = aggregate(
        blocks,
        local_cols,
        local_rows,
        live_count,
        delta_rows,
        0 // tile_size,
        column_blocks * tile_size // tile_size,
        "tji,tjf->tif",
    )
    back_summed = lax.psum_scatter(back_partial, "col", scatter_dimension=0, tiled=True)
    scaled_grad = degree_scale[:, None] * back_summed
    weight_part = jnp.dot(
        features.T, scaled_grad, precision=highest, preferred_element_type=jnp.float32
    )
    weight_total, bias_total = lax.psum((weight_part, bias_part), ("row", "col"))
    feature_grad = jnp.dot(
        scaled_grad, weight.T, precision=highest, preferred_element_type=jnp.float32
    )
    return (activation, feature_grad, weight_total * norm_factor, bias_total * norm_factor)


def solution(mesh):
    return jax.shard_map(
        local,
        mesh=mesh,
        in_specs=(
            P(("row", "col"), None),
            P(),
            P(),
            P(("row", "col")),
            P("row", "col", None, None, None),
            P("row", "col", None),
            P("row", "col"),
            P(("row", "col"), None),
        ),
        out_specs=(P(("row", "col"), None), P(("row", "col"), None), P(), P()),
        check_vma=False,
    )
```

profile of v0, /device:TPU:1, one launch (start us, length us, event | category | flops | bytes accessed | tf_op | source)
XLA Modules:
  0.0 262.1 jit_solution(9816274243464607919)
XLA Ops:
  8.6 1.0 fusion.18
  9.6 12.1 %all_gather.6 = bf16[512,128]{1,0:T(8,128)(2,1)S(1)} all-gather(bf16[128,128]{1,0:T(8,128)(2,1)S(1)} %fusion.18), channel_id=1, replica_groups=mesh['row'=8,'col'=4] {'col'}, dimensions={0}, use_global_device_ids=true | all-gather | bytes 163840 | tf_op jit(solution)/shard_map/all_gather | solution.py:71
  21.8 8.1 %while.22 = (s32[]{:T(128)}, f32[8,16384]{1,0:T(8,128)S(1)}, s32[]{:T(128)}, s32[32]{0:T(128)S(1)}, s32[]{:T(128)}, /*index=5*/s32[32]{0:T(128)S(1)}, bf16[4,128...) while((s32[]{:T(128)}, f32[8,16384]{1,0:T(8,128)S(1)}, s32[]{:T(128)}, ...), condition=%wide.region_1.2_spmd.clone, body=%wide.region_0.1_spmd.clone.sunk | while | flops 184682144 | bytes 17830740 | solution.py:48
  21.8 0.7 gather_fusion
  23.0 2.2 convolution_bitcast_fusion.5
  25.3 1.9 copy.37
  27.8 2.0 convolution_add_fusion.4
  29.9 0.9 reshape.69
  30.8 37.4 %reduce-scatter.3.cloned.1.call-done = f32[128,128]{1,0:T(8,128)} async-done(((f32[1024,128]{1,0:T(8,128)}), f32[128,128]{1,0:T(8,128)}) %reduce-scatter.3.cloned.1.call-update) | async-done | bytes 65552 | tf_op jit(solution)/shard_map/reduce_scatter | solution.py:82
  68.2 1.6 fusion.30
  69.9 10.3 %all_gather.7 = bf16[1024,128]{1,0:T(8,128)(2,1)S(1)} all-gather(bf16[128,128]{1,0:T(8,128)(2,1)S(1)} %multiply_convert_fusion), channel_id=1, replica_groups=mesh['row'=8,'col'=4] {'row'}, dimensions={0}, use_global_device_ids=true | all-gather | bytes 294912 | tf_op jit(solution)/shard_map/all_gather | solution.py:88
  80.2 0.7 broadcast_in_dim.5
  80.9 8.9 %while.23 = (s32[]{:T(128)}, f32[4,16384]{1,0:T(4,128)}, s32[]{:T(128)}, s32[32]{0:T(128)S(1)}, s32[]{:T(128)}, /*index=5*/s32[32]{0:T(128)S(1)}, bf16[8,128,128...) while((s32[]{:T(128)}, f32[4,16384]{1,0:T(4,128)}, s32[]{:T(128)}, ...), condition=%wide.region_4.5_spmd.clone, body=%wide.region_3.4_spmd.clone.sunk | while | flops 159450528 | bytes 13112121 | solution.py:48
  81.0 0.7 gather_fusion.1
  81.7 1.9 convolution_bitcast_fusion.6
  83.6 1.9 copy.39
  86.2 3.6 %convolution_add_fusion.5 = f32[4,16384]{1,0:T(4,128)} fusion(f32[4,16384]{1,0:T(4,128)} %get-tuple-element.326, f32[4,8,128,128]{3,2,1,0:T(8,128)S(1)} %bitcast.80, s32[32]{0:T(128)S(1)} %get-tuple-element.338, pred[32]{0:T(512)(128)(4,1)S(1)} %add_compare_fusion.5), kind=kOutput, calls=%fused_computation.16.clone.1 | convolution fusion | flops 25231616 | bytes 2621600 | tf_op jit(solution)/shard_map/while/body/dot_general | solution.py:40
  89.8 1.8 reshape.71
  91.7 38.0 %psum.15 = f32[128]{0:T(128)S(1)} all-reduce(f32[128]{0:T(128)S(1)} %get-tuple-element.180), channel_id=1, replica_groups=mesh['row'=8,'col'=4] {'row','col'}, use_global_device_ids=true, to_apply=%region_8.9 | all-reduce | flops 128 | bytes 1024 | tf_op jit(solution)/shard_map/psum | solution.py:104
  130.2 1.8 convolution_bitcast_fusion.2
  132.0 1.8 fusion.26
  133.8 120.2 %all-reduce.2.cloned.1.call-done = f32[128,128]{0,1:T(8,128)} async-done(((f32[128,128]{0,1:T(8,128)}), f32[128,128]{0,1:T(8,128)}) %all-reduce.2.cloned.1.call-update) | async-done | bytes 65552 | tf_op jit(solution)/shard_map/psum | solution.py:104
  254.0 0.8 broadcast_multiply_fusion
  254.8 0.7 copy.19
  (31 shorter events, 3.3 us)
Async XLA Ops:
  7.2 1.4 copy-start
  7.2 61.0 %reduce-scatter.3.cloned.1.call-start = ((), (), s32[]{:S(2)}) async-start(), calls=%async_computation.2 | async-start | bytes 589824 | tf_op jit(solution)/shard_map/reduce_scatter | solution.py:82
  21.7 46.4 %copy-start.4 = (f32[128,128]{1,0:T(8,128)S(1)}, f32[128,128]{1,0:T(8,128)}, u32[]{:S(2)}) copy-start(f32[128,128]{1,0:T(8,128)} %param.19) | copy-start | bytes 196612
  21.8 46.4 %copy-start.5 = (f32[128]{0:T(128)S(1)}, f32[128]{0:T(128)}, u32[]{:S(2)}) copy-start(f32[128]{0:T(128)} %param.15) | copy-start | bytes 1540
  21.8 46.4 %copy-start.6 = (f32[128]{0:T(128)S(1)}, f32[128]{0:T(128)}, u32[]{:S(2)}) copy-start(f32[128]{0:T(128)} %param.14) | copy-start | bytes 1540
  21.8 1.2 copy-start.1
  29.9 51.1 %copy-start.2 = (bf16[32,128,128]{2,1,0:T(8,128)(2,1)S(1)}, bf16[32,128,128]{2,1,0:T(8,128)(2,1)}, u32[]{:S(2)}) copy-start(bf16[32,128,128]{2,1,0:T(8,128)(2,1)} %get-tuple-element.348) | copy-start | bytes 3145732
  30.8 99.4 %reduce-scatter.5.cloned.1.call-start = ((), (), s32[]{:S(2)}) async-start(), calls=%async_computation.3 | async-start | bytes 327680 | tf_op jit(solution)/shard_map/reduce_scatter | solution.py:99
  80.9 51.1 %copy-start.3 = (f32[128,128]{1,0:T(8,128)S(1)}, f32[128,128]{1,0:T(8,128)}, u32[]{:S(2)}) copy-start(f32[128,128]{1,0:T(8,128)} %param.13) | copy-start | bytes 196612
  91.6 162.4 %all-reduce.2.cloned.1.call-start = ((), (), s32[]{:S(2)}) async-start(), calls=%async_computation.4 | async-start | bytes 131072 | tf_op jit(solution)/shard_map/psum | solution.py:104
Sparse Core Ops, SparseCore 0:
  30.9 37.2 reduce-scatter.2
  91.8 17.0 reduce-scatter.4
  132.1 121.7 all-reduce.1
where the time goes:
time: 263 us; the launch traced here: 262 us
  waiting for transfers between devices  158 us (60%)
  blocking collectives  60.4 us (23%)
  between operations  14.5 us (6%)
  matrix products  14.3 us (5%)
  local copies, waits for them, and re-layouts  10 us (4%)
  other arithmetic  5.02 us (2%)
    psum x1, waiting for transfers between devices, local(): lax.psum((weight_part, bias_part), ('row', 'col'))  120 us
    psum x1, blocking collectives, local(): lax.psum((weight_part, bias_part), ('row', 'col'))  38 us
    reduce_scatter x1, waiting for transfers between devices, local(): lax.psum_scatter(partial_value, 'row', scatter_dimension=0, tiled=True)  37.4 us
    all_gather x1, blocking collectives, local(): gathered = lax.all_gather(scaled, 'col', axis=0, tiled=True)  12.1 us
    all_gather x1, blocking collectives, local(): delta_rows = lax.all_gather(delta_scaled, 'row', axis=0, tiled=True)  10.3 us
    dot_general x2, matrix products, accumulate(): jnp.dot(selector, products.reshape(TBLK, tile_size * feature_width), prec...  5.6 us
  transfers between devices with their start and end apart: 3, of which 2 were waited for; matrix products, arithmetic and copies ran while one was open for 1% of the time, Pallas kernels for 0%

commit v1 on v0

--- a/solution.py
+++ b/solution.py
@@ -5,6 +5,10 @@
 from jax.sharding import PartitionSpec as P
 
 TBLK = 32
+
+
+def _group_tables(local_values):
+    return jax.lax.psum(jax.lax.psum(local_values, "col"), "row")
 
 
 def gelu_pair(values):
@@ -101,7 +105,7 @@
     weight_part = jnp.dot(
         features.T, scaled_grad, precision=highest, preferred_element_type=jnp.float32
     )
-    weight_total, bias_total = lax.psum((weight_part, bias_part), ("row", "col"))
+    weight_total, bias_total = _group_tables((weight_part, bias_part))
     feature_grad = jnp.dot(
         scaled_grad, weight.T, precision=highest, preferred_element_type=jnp.float32
     )

time: 263 us -> 213 us (0.81)
  waiting for transfers between devices: 158 us -> 120 us
  blocking collectives: 60.4 us -> 45.9 us
    psum x1 -> x2, waiting for transfers between devices: 120 us -> 82.9 us  [_group_tables(): return jax.lax.psum(jax.lax.psum(local_values, 'col'), 'row')]
    psum x1 -> x2, blocking collectives: 38 us -> 23.5 us  [_group_tables(): return jax.lax.psum(jax.lax.psum(local_values, 'col'), 'row')]
  transfers between devices with their start and end apart: 3 -> 4, of which waited for: 2 -> 3; matrix products, arithmetic and copies ran while one was open for 1% -> 1% of each run, Pallas kernels for 0% -> 0%
where the time goes in v1:
time: 213 us; the launch traced here: 210 us
  waiting for transfers between devices  120 us (56%)
  blocking collectives  45.9 us (22%)
  between operations  14.5 us (7%)
  matrix products  14.3 us (7%)
  local copies, waits for them, and re-layouts  10 us (5%)
  other arithmetic  5.02 us (2%)
    psum x2, waiting for transfers between devices, _group_tables(): return jax.lax.psum(jax.lax.psum(local_values, 'col'), 'row')  82.9 us
    reduce_scatter x1, waiting for transfers between devices, local(): lax.psum_scatter(partial_value, 'row', scatter_dimension=0, tiled=True)  37.4 us
    psum x2, blocking collectives, _group_tables(): return jax.lax.psum(jax.lax.psum(local_values, 'col'), 'row')  23.5 us
    all_gather x1, blocking collectives, local(): gathered = lax.all_gather(scaled, 'col', axis=0, tiled=True)  12.1 us
    all_gather x1, blocking collectives, local(): delta_rows = lax.all_gather(delta_scaled, 'row', axis=0, tiled=True)  10.3 us
    dot_general x2, matrix products, accumulate(): jnp.dot(selector, products.reshape(TBLK, tile_size * feature_width), prec...  5.62 us
  transfers between devices with their start and end apart: 4, of which 3 were waited for; matrix products, arithmetic and copies ran while one was open for 1% of the time, Pallas kernels for 0%

profile of v1, /device:TPU:1, one launch (start us, length us, event | category | flops | bytes accessed | tf_op | source)
XLA Modules:
  0.0 210.4 jit_solution(3515346471663710258)
XLA Ops:
  8.6 1.0 fusion.18
  9.6 12.1 %all_gather.6 = bf16[512,128]{1,0:T(8,128)(2,1)S(1)} all-gather(bf16[128,128]{1,0:T(8,128)(2,1)S(1)} %fusion.18), channel_id=1, replica_groups=mesh['row'=8,'col'=4] {'col'}, dimensions={0}, use_global_device_ids=true | all-gather | bytes 163840 | tf_op jit(solution)/shard_map/all_gather | solution.py:75
  21.8 8.1 %while.22 = (s32[]{:T(128)}, f32[8,16384]{1,0:T(8,128)S(1)}, s32[]{:T(128)}, s32[32]{0:T(128)S(1)}, s32[]{:T(128)}, /*index=5*/s32[32]{0:T(128)S(1)}, bf16[4,128...) while((s32[]{:T(128)}, f32[8,16384]{1,0:T(8,128)S(1)}, s32[]{:T(128)}, ...), condition=%wide.region_1.2_spmd.clone, body=%wide.region_0.1_spmd.clone.sunk | while | flops 184682144 | bytes 17830740 | solution.py:52
  21.8 0.7 gather_fusion
  23.0 2.2 %convolution_bitcast_fusion.5 = f32[32,128,128]{1,2,0:T(8,128)} fusion(bf16[32,128,128]{2,1,0:T(8,128)(2,1)S(1)} %gather_fusion, bf16[32,128,128]{2,1,0:T(8,128)(2,1)S(1)} %copy-done.1), kind=kOutput, calls=%fused_computation.7.clone.1 | convolution fusion | flops 134217728 | bytes 4194304 | tf_op jit(solution)/shard_map/while/body/tij,tjf->tif/dot_general | solution.py:39
  25.3 1.9 copy.37
  27.8 2.0 convolution_add_fusion.4
  29.9 0.9 reshape.69
  30.8 37.4 %reduce-scatter.3.cloned.1.call-done = f32[128,128]{1,0:T(8,128)} async-done(((f32[1024,128]{1,0:T(8,128)}), f32[128,128]{1,0:T(8,128)}) %reduce-scatter.3.cloned.1.call-update) | async-done | bytes 65552 | tf_op jit(solution)/shard_map/reduce_scatter | solution.py:86
  68.2 1.6 fusion.30
  69.9 10.3 %all_gather.7 = bf16[1024,128]{1,0:T(8,128)(2,1)S(1)} all-gather(bf16[128,128]{1,0:T(8,128)(2,1)S(1)} %multiply_convert_fusion), channel_id=1, replica_groups=mesh['row'=8,'col'=4] {'row'}, dimensions={0}, use_global_device_ids=true | all-gather | bytes 294912 | tf_op jit(solution)/shard_map/all_gather | solution.py:92
  80.2 0.8 broadcast_in_dim.5
  80.9 8.9 %while.23 = (s32[]{:T(128)}, f32[4,16384]{1,0:T(4,128)}, s32[]{:T(128)}, s32[32]{0:T(128)S(1)}, s32[]{:T(128)}, /*index=5*/s32[32]{0:T(128)S(1)}, bf16[8,128,128...) while((s32[]{:T(128)}, f32[4,16384]{1,0:T(4,128)}, s32[]{:T(128)}, ...), condition=%wide.region_4.5_spmd.clone, body=%wide.region_3.4_spmd.clone.sunk | while | flops 159450528 | bytes 13112121 | solution.py:52
  81.7 1.9 convolution_bitcast_fusion.6
  83.6 1.9 copy.39
  86.2 3.6 %convolution_add_fusion.5 = f32[4,16384]{1,0:T(4,128)} fusion(f32[4,16384]{1,0:T(4,128)} %get-tuple-element.326, f32[4,8,128,128]{3,2,1,0:T(8,128)S(1)} %bitcast.80, s32[32]{0:T(128)S(1)} %get-tuple-element.338, pred[32]{0:T(512)(128)(4,1)S(1)} %add_compare_fusion.5), kind=kOutput, calls=%fused_computation.16.clone.1 | convolution fusion | flops 25231616 | bytes 2621600 | tf_op jit(solution)/shard_map/while/body/dot_general | solution.py:44
  89.8 1.8 reshape.71
  91.7 9.7 %psum.30 = f32[128]{0:T(128)S(1)} all-reduce(f32[128]{0:T(128)S(1)} %get-tuple-element.180), channel_id=1, replica_groups=mesh['row'=8,'col'=4] {'col'}, use_global_device_ids=true, to_apply=%region_9.10 | all-reduce | flops 128 | bytes 1024 | tf_op jit(solution)/shard_map/psum | solution.py:11
  101.4 13.8 %psum.31 = f32[128]{0:T(128)S(1)} all-reduce(f32[128]{0:T(128)S(1)} %psum.30), channel_id=1, replica_groups=mesh['row'=8,'col'=4] {'row'}, use_global_device_ids=true, to_apply=%region_10.11 | all-reduce | flops 128 | bytes 1024 | tf_op jit(solution)/shard_map/psum | solution.py:11
  115.2 1.8 convolution_bitcast_fusion.2
  117.6 27.6 %all-reduce.3.cloned.1.call-done = f32[128,128]{0,1:T(8,128)} async-done(((f32[128,128]{0,1:T(8,128)}), f32[128,128]{0,1:T(8,128)}) %all-reduce.3.cloned.1.call-update) | async-done | bytes 65552 | tf_op jit(solution)/shard_map/psum | solution.py:11
  145.3 1.8 fusion.26
  147.1 55.3 %all-reduce.5.cloned.1.call-done = f32[128,128]{0,1:T(8,128)} async-done(((f32[128,128]{0,1:T(8,128)}), f32[128,128]{0,1:T(8,128)}) %all-reduce.5.cloned.1.call-update) | async-done | bytes 65552 | tf_op jit(solution)/shard_map/psum | solution.py:11
  202.3 0.8 broadcast_multiply_fusion
  (35 shorter events, 4.8 us)
Async XLA Ops:
  7.2 1.4 copy-start
  7.2 61.0 %reduce-scatter.3.cloned.1.call-start = ((), (), s32[]{:S(2)}) async-start(), calls=%async_computation.2 | async-start | bytes 589824 | tf_op jit(solution)/shard_map/reduce_scatter | solution.py:86
  21.7 46.4 %copy-start.4 = (f32[128,128]{1,0:T(8,128)S(1)}, f32[128,128]{1,0:T(8,128)}, u32[]{:S(2)}) copy-start(f32[128,128]{1,0:T(8,128)} %param.19) | copy-start | bytes 196612
  21.8 46.4 %copy-start.5 = (f32[128]{0:T(128)S(1)}, f32[128]{0:T(128)}, u32[]{:S(2)}) copy-start(f32[128]{0:T(128)} %param.15) | copy-start | bytes 1540
  21.8 46.4 %copy-start.6 = (f32[128]{0:T(128)S(1)}, f32[128]{0:T(128)}, u32[]{:S(2)}) copy-start(f32[128]{0:T(128)} %param.14) | copy-start | bytes 1540
  21.8 1.2 copy-start.1
  29.8 51.1 %copy-start.2 = (bf16[32,128,128]{2,1,0:T(8,128)(2,1)S(1)}, bf16[32,128,128]{2,1,0:T(8,128)(2,1)}, u32[]{:S(2)}) copy-start(bf16[32,128,128]{2,1,0:T(8,128)(2,1)} %get-tuple-element.349) | copy-start | bytes 3145732
  30.8 84.5 %reduce-scatter.5.cloned.1.call-start = ((), (), s32[]{:S(2)}) async-start(), calls=%async_computation.3 | async-start | bytes 327680 | tf_op jit(solution)/shard_map/reduce_scatter | solution.py:103
  80.9 64.3 %copy-start.3 = (f32[128,128]{1,0:T(8,128)S(1)}, f32[128,128]{1,0:T(8,128)}, u32[]{:S(2)}) copy-start(f32[128,128]{1,0:T(8,128)} %param.13) | copy-start | bytes 196612
  91.7 53.6 %all-reduce.3.cloned.1.call-start = ((), (), s32[]{:S(2)}) async-start(), calls=%async_computation.4 | async-start | bytes 131072 | tf_op jit(solution)/shard_map/psum | solution.py:11
  117.1 85.3 %all-reduce.5.cloned.1.call-start = ((), (), s32[]{:S(2)}) async-start(), calls=%async_computation.5 | async-start | bytes 131072 | tf_op jit(solution)/shard_map/psum | solution.py:11
Sparse Core Ops, SparseCore 0:
  30.9 37.2 reduce-scatter.2
  91.8 17.1 reduce-scatter.4
  117.2 28.0 all-reduce.2
  148.2 54.1 all-reduce.4
